TPU v7x, 256 devices: a whole 4x4x8 slice. The times are simulated.
256 devices in a mesh: pair: 64 (over y, z, core), red: 4 (over x).
Axes of the slice: x: 4, y: 4, z: 8, core: 2. Of those that a mesh axis runs over, the one named last changes fastest.
Arguments:
- amplitudes: bfloat16 [64, 64, 8192], P('pair', None, 'red'), may hold values from -6 to 6
- integrals: bfloat16 [8192, 8192], P('red'), may hold values from -0.1875 to 0.1875
- occ_irrep: int32 [64], replicated, may hold values from 0 to 7
- vir_irrep: int32 [512], replicated, may hold values from 0 to 7, as said below
- cd_orbitals: int32 [2, 8192], P(None, 'red'), may hold values from 0 to 511
- ab_orbitals: int32 [2, 8192], P(None, 'pair'), may hold values from 0 to 511, as said below
Outputs:
- residual: bfloat16 [64, 64, 8192], P(None, 'red', 'pair')
Inputs may be any that keep to these rules, and one draw needn't show every extreme that they name: `vir_irrep`: D2h irrep labels; each label is held by exactly 64 virtual orbitals. `occ_irrep`: D2h irrep labels. `cd_orbitals`: indices of virtual orbitals. `ab_orbitals`: indices of virtual orbitals; the slab pairs m with m // 128 equal come as 8 blocks of 16 pairs, and ab_irrep[m] = (m % 128) // 16.
All inputs are finite; a program needn't handle non-finite values.
Results may differ from a plain program's by a relative error of at most 0.001.
Values may be sent and summed in bfloat16 or wider, within the bound.
A program may use at most 192 MiB of HBM per device.

v0:
```python
import jax
import jax.numpy as jnp
from jax import lax
from jax.sharding import PartitionSpec as P


def pair_labels(orbitals, vir_irrep):
    labels = lax.broadcasted_iota(jnp.int32, (1, vir_irrep.shape[0]), 1)
    first_label = jnp.sum(jnp.where(orbitals[0][:, None] == labels, vir_irrep[None, :], 0), axis=1)
    second_label = jnp.sum(jnp.where(orbitals[1][:, None] == labels, vir_irrep[None, :], 0), axis=1)
    return jnp.bitwise_xor(first_label, second_label)


def local(amplitudes, integrals, occ_irrep, vir_irrep, cd_orbitals, ab_orbitals):
    own_rows = amplitudes.shape[0]
    occupied = amplitudes.shape[1]
    slab_width = integrals.shape[1]
    first_row = lax.axis_index("pair") * own_rows
    own_irrep = lax.dynamic_slice_in_dim(occ_irrep, first_row, own_rows, 0)
    pair_irrep = jnp.bitwise_xor(own_irrep[:, None], occ_irrep[None, :])
    cd_irrep = pair_labels(cd_orbitals, vir_irrep)
    masked = jnp.where(
        pair_irrep[:, :, None] == cd_irrep[None, None, :],
        amplitudes,
        jnp.zeros((), amplitudes.dtype),
    )
    partial_sums = jnp.dot(
        masked.reshape(own_rows * occupied, masked.shape[2]),
        integrals,
        preferred_element_type=jnp.float32,
    )
    partial_sums = partial_sums.reshape(own_rows, occupied, slab_width)
    moved = lax.all_to_all(partial_sums, "pair", split_axis=2, concat_axis=0, tiled=True)
    summed = lax.psum_scatter(moved, "red", scatter_dimension=1, tiled=True)
    j_rows = summed.shape[1]
    j_irrep = lax.dynamic_slice_in_dim(occ_irrep, lax.axis_index("red") * j_rows, j_rows, 0)
    out_irrep = jnp.bitwise_xor(occ_irrep[:, None], j_irrep[None, :])
    ab_irrep = pair_labels(ab_orbitals, vir_irrep)
    kept = jnp.where(
        out_irrep[:, :, None] == ab_irrep[None, None, :], summed, jnp.zeros((), summed.dtype)
    )
    return kept.astype(jnp.bfloat16)


def solution(mesh):
    in_specs = (P("pair", None, "red"), P("red", None), P(), P(), P(None, "red"), P(None, "pair"))
    out_specs = P(None, "red", "pair")
    return jax.shard_map(local, mesh=mesh, in_specs=in_specs, out_specs=out_specs, check_vma=False)
```

profile of v0, /device:TPU:1, one launch (start us, length us, event | category | flops | bytes accessed | tf_op | source)
XLA Modules:
  0.0 194.9 jit_solution(4072649862004780560)
XLA Ops:
  6.5 0.0 reduce-scatter.2.cloned.1.call-start
  6.5 1.2 dynamic_slice.7
  7.8 1.3 broadcast_xor_fusion.1
  9.1 0.8 fusion.7
  9.9 2.3 %select_reduce_fusion = (s32[2048]{0:T(1024)S(1)}, s32[2048]{0:T(1024)S(1)}) fusion(s32[2048]{0:T(1024)S(1)} %bitcast.23, s32[512]{0:T(512)} %param.9, s32[2048]{0:T(1024)S(1)} %bitcast.22), kind=kLoop, calls=%fused_computation | loop fusion | flops 6287360 | bytes 34816 | tf_op jit(solution)/shard_map/reduce_sum | solution.py:10
  12.2 19.2 %fusion.1 = f32[64,8192]{0,1:T(8,128)} fusion(bf16[2048,8192]{1,0:T(8,128)(2,1)} %param.7, bf16[1,64,2048]{2,1,0:T(8,128)(2,1)} %param.6, s32[2048]{0:T(1024)S(1)} %xor.49, s32[64]{0:T(128)S(1)} %broadcast_xor_fusion.1), kind=kOutput, calls=%fused_computation.7 | convolution fusion | flops 2147745792 | bytes 35922176 | tf_op jit(solution)/shard_map/dot_general | solution.py:27
  31.4 0.5 broadcast.63
  32.0 38.4 %reduce = f32[8192,64]{1,0:T(8,128)} reduce(f32[8192,1,64]{2,1,0:T(1,128)} %bitcast.19, f32[]{:T(128)} %broadcast.63), dimensions={1}, to_apply=%bitcast.16.reduce_sub_computation | reduce | bytes 4194308
  70.4 4.6 %reshape.102 = f32[64,1,8192]{2,1,0:T(1,128)S(1)} reshape(f32[8192,64]{1,0:T(8,128)} %reduce) | data formatting | bytes 4194304
  74.9 64.3 %all_to_all.18 = f32[64,1,8192]{2,1,0:T(1,128)} all-to-all(f32[64,1,8192]{2,1,0:T(1,128)S(1)} %reshape.102), channel_id=1, replica_groups=mesh['pair'=64,'red'=4] {'pair'}, dimensions={0} | all-to-all | bytes 4194304 | tf_op jit(solution)/shard_map/all_to_all | solution.py:33
  139.2 7.5 %reduce.1 = f32[64,8192]{1,0:T(8,128)S(1)} reduce(f32[64,1,8192]{2,1,0:T(1,128)} %all_to_all.18, f32[]{:T(128)} %broadcast.63), dimensions={1}, to_apply=%all_to_all.13.reduce_sub_computation | reduce | bytes 4194308 | tf_op jit(solution)/shard_map/all_to_all | solution.py:33
  146.8 6.6 %reshape.103 = f32[8192,1,64]{2,1,0:T(1,128)} reshape(f32[64,8192]{1,0:T(8,128)S(1)} %reduce.1) | data formatting | bytes 4194304
  153.4 0.0 copy-start.2
  153.4 0.0 copy-start.1
  153.4 0.0 copy-start
  153.4 3.9 %copy.11 = f32[1,64,64,128]{3,1,2,0:T(8,128)} copy(f32[1,64,64,128]{1,3,2,0:T(8,128)} %bitcast.20) | data formatting | bytes 4194304 | tf_op jit(solution)/shard_map/all_to_all | solution.py:33
  157.2 0.0 reduce-scatter.2.cloned.1.call-update
  157.3 0.0 copy-done.2
  157.3 0.1 dynamic_slice.6
  157.3 0.0 copy-done.1
  157.3 0.0 copy-done
  157.4 0.2 select_reduce_fusion.2
  157.6 0.1 broadcast_xor_fusion
  157.6 28.5 %reduce-scatter.2.cloned.1.call-done = f32[64,16,128]{2,1,0:T(8,128)} async-done(((f32[64,64,128]{2,1,0:T(8,128)}), f32[64,16,128]{2,1,0:T(8,128)}) %reduce-scatter.2.cloned.1.call-update) | async-done | bytes 524304 | tf_op jit(solution)/shard_map/reduce_scatter | solution.py:34
  186.1 1.9 select_convert_fusion
  (3 shorter events, 0.0 us)
Async XLA Ops:
  6.5 179.6 %reduce-scatter.2.cloned.1.call-start = ((), (), s32[]{:S(2)}) async-start(), calls=%async_computation.2 | async-start | bytes 2621440 | tf_op jit(solution)/shard_map/reduce_scatter | solution.py:34
  153.4 3.9 %copy-start.2 = (s32[64]{0:T(128)S(1)}, s32[64]{0:T(128)}, u32[]{:S(2)}) copy-start(s32[64]{0:T(128)} %param.8) | copy-start | bytes 772
  153.4 4.0 %copy-start.1 = (s32[2,128]{1,0:T(2,128)S(1)}, s32[2,128]{1,0:T(2,128)}, u32[]{:S(2)}) copy-start(s32[2,128]{1,0:T(2,128)} %param.11) | copy-start | bytes 3076
  153.4 4.0 %copy-start = (s32[512]{0:T(512)S(1)}, s32[512]{0:T(512)}, u32[]{:S(2)}) copy-start(s32[512]{0:T(512)} %param.9) | copy-start | bytes 6148
Sparse Core Ops, SparseCore 0:
  157.4 28.6 reduce-scatter.1
where the time goes:
time: 195 us
  blocking collectives  64.3 us (33%)
  other arithmetic  51.8 us (27%)
  waiting for transfers between devices  28.5 us (15%)
  matrix products  19.2 us (10%)
  local copies, waits for them, and re-layouts  17.6 us (9%)
  between operations  13.5 us (7%)
    all_to_all x1, blocking collectives, local(): lax.all_to_all(partial_sums, 'pair', split_axis=2, concat_axis=0, tiled=T...  64.3 us
    unnamed x1, other arithmetic  38.4 us
    reduce_scatter x1, waiting for transfers between devices, local(): summed = lax.psum_scatter(moved, 'red', scatter_dimension=1, tiled=True)  28.5 us
    dot_general x1, matrix products, local(): jnp.dot(masked.reshape(own_rows * occupied, masked.shape[2]), integrals,...  19.2 us
    unnamed x9, local copies, waits for them, and re-layouts  11.6 us
    all_to_all x1, other arithmetic, local(): lax.all_to_all(partial_sums, 'pair', split_axis=2, concat_axis=0, tiled=T...  7.54 us
  transfers between devices with their start and end apart: 1, of which 1 were waited for; matrix products, arithmetic and copies ran while one was open for 0% of the time, Pallas kernels for 0%

commit v1 on v0

--- a/solution.py
+++ b/solution.py
@@ -2,6 +2,13 @@
 import jax.numpy as jnp
 from jax import lax
 from jax.sharding import PartitionSpec as P
+
+
+def swap_blocks(array, axis, split, join):
+    size = lax.axis_size(axis)
+    tiles = jnp.stack(jnp.split(array, size, axis=split), axis=0)
+    tiles = lax.all_to_all(tiles, axis, split_axis=0, concat_axis=0)
+    return jnp.concatenate(tiles, axis=join)
 
 
 def pair_labels(orbitals, vir_irrep):
@@ -30,7 +37,7 @@
         preferred_element_type=jnp.float32,
     )
     partial_sums = partial_sums.reshape(own_rows, occupied, slab_width)
-    moved = lax.all_to_all(partial_sums, "pair", split_axis=2, concat_axis=0, tiled=True)
+    moved = swap_blocks(partial_sums, "pair", 2, 0)
     summed = lax.psum_scatter(moved, "red", scatter_dimension=1, tiled=True)
     j_rows = summed.shape[1]
     j_irrep = lax.dynamic_slice_in_dim(occ_irrep, lax.axis_index("red") * j_rows, j_rows, 0)

time: 195 us -> 129 us (0.66)
  other arithmetic: 51.8 us -> 5.84 us
  local copies, waits for them, and re-layouts: 17.6 us -> 3.19 us
  matrix products: 19.2 us -> 13.8 us
    unnamed x1 -> x0, other arithmetic: 38.4 us -> none
    unnamed x9 -> x69, local copies, waits for them, and re-layouts: 11.6 us -> 1.06 us
    all_to_all x1 -> x0, other arithmetic: 7.54 us -> none  [local(): lax.all_to_all(partial_sums, 'pair', split_axis=2, concat_axis=0, tiled=T...]
    dot_general x1, matrix products: 19.2 us -> 13.8 us  [local(): jnp.dot(masked.reshape(own_rows * occupied, masked.shape[2]), integrals,...]
    all_to_all x1 -> x0, local copies, waits for them, and re-layouts: 3.87 us -> none  [local(): lax.all_to_all(partial_sums, 'pair', split_axis=2, concat_axis=0, tiled=T...]
where the time goes in v1:
time: 129 us
  blocking collectives  64.3 us (50%)
  waiting for transfers between devices  27.9 us (22%)
  between operations  13.9 us (11%)
  matrix products  13.8 us (11%)
  other arithmetic  5.84 us (5%)
  local copies, waits for them, and re-layouts  3.19 us (2%)
    all_to_all x1, blocking collectives, swap_blocks(): tiles = lax.all_to_all(tiles, axis, split_axis=0, concat_axis=0)  64.3 us
    reduce_scatter x1, waiting for transfers between devices, local(): summed = lax.psum_scatter(moved, 'red', scatter_dimension=1, tiled=True)  27.9 us
    dot_general x1, matrix products, local(): jnp.dot(masked.reshape(own_rows * occupied, masked.shape[2]), integrals,...  13.8 us
  transfers between devices with their start and end apart: 1, of which 1 were waited for; matrix products, arithmetic and copies ran while one was open for 0% of the time, Pallas kernels for 0%

profile of v1, /device:TPU:1, one launch (start us, length us, event | category | flops | bytes accessed | tf_op | source)
XLA Modules:
  0.0 129.0 jit_solution(4237532948766741359)
XLA Ops:
  6.5 0.0 reduce-scatter.2.cloned.1.call-start
  6.5 1.2 dynamic_slice.7
  7.8 1.3 %broadcast_xor_fusion.1 = s32[64]{0:T(128)S(1)} fusion(s32[64]{0:T(128)} %param.8, s32[]{:T(128)} %bitcast.2), kind=kLoop, calls=%fused_computation.146 | loop fusion | flops 64 | bytes 516 | tf_op jit(solution)/shard_map/xor | solution.py:27
  9.1 0.8 fusion.6
  9.9 2.3 %select_reduce_fusion = (s32[2048]{0:T(1024)S(1)}, s32[2048]{0:T(1024)S(1)}) fusion(s32[2048]{0:T(1024)S(1)} %bitcast.272, s32[512]{0:T(512)} %param.9, s32[2048]{0:T(1024)S(1)} %bitcast.271), kind=kLoop, calls=%fused_computation.1 | loop fusion | flops 6287360 | bytes 34816 | tf_op jit(solution)/shard_map/reduce_sum | solution.py:17
  12.2 13.8 %convolution_bitcast_fusion = f32[1,64,8192]{2,1,0:T(8,128)S(1)} fusion(bf16[2048,8192]{1,0:T(8,128)(2,1)} %param.7, bf16[1,64,2048]{2,1,0:T(8,128)(2,1)} %param.6, s32[2048]{0:T(1024)S(1)} %xor.49, s32[64]{0:T(128)S(1)} %broadcast_xor_fusion.1), kind=kOutput, calls=%fused_computation | convolution fusion | flops 2147745792 | bytes 35922176 | tf_op jit(solution)/shard_map/dot_general | solution.py:34
  26.9 64.3 %all_to_all.5 = f32[64,1,64,128]{3,2,1,0:T(8,128)} all-to-all(f32[64,1,64,128]{3,2,1,0:T(8,128)S(1)} %constant_dynamic-update-slice_fusion), channel_id=1, replica_groups=mesh['pair'=64,'red'=4] {'pair'}, dimensions={0} | all-to-all | bytes 4194304 | tf_op jit(solution)/shard_map/all_to_all | solution.py:10
  91.3 0.0 copy-start.2
  91.3 0.0 copy-start.1
  91.3 0.0 copy-start
  91.3 0.0 reduce-scatter.2.cloned.1.call-update
  91.3 0.6 copy-done.2
  91.9 0.1 dynamic_slice.6
  92.0 0.0 copy-done.1
  92.0 0.0 copy-done
  92.0 0.2 select_reduce_fusion.2
  92.2 0.1 broadcast_xor_fusion
  92.3 27.9 %reduce-scatter.2.cloned.1.call-done = f32[64,16,128]{2,1,0:T(8,128)} async-done(((f32[64,64,128]{2,1,0:T(8,128)}), f32[64,16,128]{2,1,0:T(8,128)}) %reduce-scatter.2.cloned.1.call-update) | async-done | bytes 524304 | tf_op jit(solution)/shard_map/reduce_scatter | solution.py:41
  120.2 1.9 %select_convert_fusion = bf16[64,16,128]{2,1,0:T(8,128)(2,1)} fusion(f32[64,16,128]{2,1,0:T(8,128)} %reduce-scatter.2.cloned.1.call-done, s32[128]{0:T(128)S(1)} %xor.45, s32[64,16]{1,0:T(8,128)S(1)} %broadcast_xor_fusion), kind=kLoop, calls=%fused_computation.5 | loop fusion | flops 262144 | bytes 791040 | tf_op jit(solution)/shard_map/convert_element_type | solution.py:49
  (67 shorter events, 0.5 us)
Async XLA Ops:
  6.5 113.6 %reduce-scatter.2.cloned.1.call-start = ((), (), s32[]{:S(2)}) async-start(), calls=%async_computation.2 | async-start | bytes 2621440 | tf_op jit(solution)/shard_map/reduce_scatter | solution.py:41
  91.3 0.7 copy-start.2
  91.3 0.7 copy-start.1
  91.3 0.7 copy-start
Sparse Core Ops, SparseCore 0:
  91.4 28.7 reduce-scatter.1
